TPU v7x, 256 devices: a whole 4x4x8 slice. The times are simulated.
256 devices in a mesh: seq: 32 (over y_hi, z, core), head: 8 (over x, y_lo).
Axes of the slice: x: 4, y: 4 (y_hi: 2, y_lo: 2; y = y_hi * 2 + y_lo), z: 8, core: 2. Of those that a mesh axis runs over, the one named last changes fastest.
Arguments:
- resid: bfloat16 [8192, 8192], P('seq'), may hold values from -6 to 6
- norm_gain: float32 [8192], replicated, may hold values from 0.1 to 1.9
- sender_diff: bfloat16 [8192, 4096], P('seq', 'head'), may hold values from -6 to 6
- w_out1: bfloat16 [4096, 8192], P('head', 'seq'), may hold values from -0.09375 to 0.09375
- w_query: bfloat16 [8192, 4096], P('seq', 'head')
- w_key: bfloat16 [8192, 1024], P('seq', 'head')
- w_value: bfloat16 [8192, 1024], P('seq', 'head'), may hold values from -0.0625 to 0.0625
- edge_mask: int32 [32, 32], replicated, may hold values 0 or 1
- doc_ids: int32 [32, 256], P('seq'), may hold values from 0 to 3, never falling along the last dimension, each value on 1 to 128 neighbouring positions
Outputs:
- patched: bfloat16 [8192, 4096], P('seq', 'head')
All inputs are finite; a program needn't handle non-finite values.
Results may differ from a plain program's by a relative error of at most 0.0085.
The roundings to bfloat16 on the way count: a program that leaves them out, or rounds other values in their place, can miss the bound.
Values may be sent and summed in bfloat16 or wider, within the bound.
A program may use at most 128 MiB of HBM per device.

v0:
```python
import jax
import jax.numpy as jnp
from jax import lax
from jax.sharding import PartitionSpec as P

HEAD_SIZE = 128
epsilon = 1e-05


def attend(query, keys, values, doc_row, head_dim):
    tokens = query.shape[0]
    groups = keys.shape[1] // head_dim
    query_head_rows = query.reshape(tokens, groups, -1, head_dim)
    key_head_rows = keys.reshape(tokens, groups, head_dim)
    value_head_rows = values.reshape(tokens, groups, head_dim)
    attention_scores = jnp.einsum(
        "pehm,qem->ehpq", query_head_rows, key_head_rows, preferred_element_type=jnp.float32
    ) * head_dim ** (-0.5)
    position = jnp.arange(tokens, dtype=jnp.int32)
    allowed = (doc_row[:, None] == doc_row[None, :]) & (position[None, :] <= position[:, None])
    attention_scores = jnp.where(allowed, attention_scores, -jnp.inf)
    top = jnp.max(attention_scores, axis=-1, keepdims=True)
    attention_weights = jnp.exp(attention_scores - top)
    attention_weights = (
        attention_weights / jnp.sum(attention_weights, axis=-1, keepdims=True)
    ).astype(jnp.bfloat16)
    mixed_values = jnp.einsum(
        "uczp,puv->zucv", attention_weights, value_head_rows, preferred_element_type=jnp.float32
    )
    return mixed_values.astype(jnp.bfloat16).reshape(tokens, -1)


def local(resid, norm_gain, sender_diff, w_out1, w_query, w_key, w_value, edge_mask, doc_ids):
    head_dim = HEAD_SIZE
    query_cols = w_query.shape[1]
    resid_wide = resid.astype(jnp.float32)
    inv_rms = lax.rsqrt(jnp.mean(resid_wide * resid_wide, axis=1) + epsilon)
    normed = (resid_wide * inv_rms[:, None] * norm_gain[None, :]).astype(jnp.bfloat16)
    seq_index = lax.axis_index("seq")
    head_index = lax.axis_index("head")
    receivers = query_cols // head_dim
    senders = edge_mask.shape[0]
    local_mask = lax.dynamic_slice_in_dim(edge_mask, head_index * receivers, receivers, 1).astype(
        jnp.float32
    )
    clean_query = jnp.dot(
        normed,
        lax.all_gather(w_query, "seq", axis=0, tiled=True),
        preferred_element_type=jnp.float32,
    )
    keys = jnp.dot(
        normed, lax.all_gather(w_key, "seq", axis=0, tiled=True), preferred_element_type=jnp.float32
    ).astype(jnp.bfloat16)
    values = jnp.dot(
        normed,
        lax.all_gather(w_value, "seq", axis=0, tiled=True),
        preferred_element_type=jnp.float32,
    ).astype(jnp.bfloat16)
    sender_all = lax.all_gather(sender_diff, "head", axis=1, tiled=True)
    rows_dev = w_query.shape[0]
    gain_rows = lax.dynamic_slice_in_dim(norm_gain, seq_index * rows_dev, rows_dev)
    scaled = (w_query.astype(jnp.float32) * gain_rows[:, None]).astype(jnp.bfloat16)
    partial_virtual = jnp.dot(
        lax.all_gather(w_out1, "head", axis=0, tiled=True),
        scaled,
        preferred_element_type=jnp.float32,
    )
    partial_virtual = (
        partial_virtual.reshape(senders, head_dim, receivers, head_dim)
        * local_mask[:, None, :, None]
    ).reshape(senders * head_dim, query_cols)
    virtual = lax.psum(partial_virtual, "seq").astype(jnp.bfloat16)
    delta = jnp.dot(sender_all, virtual, preferred_element_type=jnp.float32)
    query = (clean_query + inv_rms[:, None] * delta).astype(jnp.bfloat16)
    return attend(query, keys, values, doc_ids[0], head_dim)


def solution(mesh):
    placed = (
        P("seq", None),
        P(),
        P("seq", "head"),
        P("head", "seq"),
        P("seq", "head"),
        P("seq", "head"),
        P("seq", "head"),
        P(),
        P("seq", None),
    )
    return jax.shard_map(
        local, mesh=mesh, in_specs=placed, out_specs=P("seq", "head"), check_vma=False
    )
```

profile of v0, /device:TPU:1, one launch (start us, length us, event | category | flops | bytes accessed | tf_op | source)
XLA Modules:
  0.0 447.9 jit_solution(1219935657815322950)
XLA Ops:
  6.5 0.7 all-gather.12.cloned.1.call-update
  7.3 0.7 all-gather.10.cloned.1.call-update
  8.1 0.7 all-gather.14.cloned.1.call-update
  8.8 0.5 all-gather.8.cloned.1.call-update
  9.4 0.5 all-gather.6.cloned.1.call-update
  9.9 0.1 constant_dynamic-slice_fusion
  10.0 0.1 copy.22
  10.1 3.1 fusion
  13.2 0.1 fusion.30
  13.3 0.1 dynamic_slice.6
  13.4 52.5 %all-gather.12.cloned.1.call-done = bf16[4096,256]{1,0:T(8,128)(2,1)} async-done(((bf16[512,256]{1,0:T(8,128)(2,1)}), bf16[4096,256]{1,0:T(8,128)(2,1)}) %all-gather.12.cloned.1.call-update) | async-done | bytes 2097168 | tf_op jit(solution)/shard_map/all_gather | solution.py:64
  65.9 1.1 mul.77
  67.1 0.4 copy-done.1
  67.5 9.2 %bitcast_multiply_fusion = f32[4096,512]{0,1:T(8,128)} fusion(f32[64,8,32,128]{3,2,1,0:T(8,128)S(1)} %bitcast.54, bf16[4096,256]{1,0:T(8,128)(2,1)S(1)} %copy-done.1, bf16[256,512]{1,0:T(8,128)(2,1)S(1)} %copy-done.2, f32[256]{0:T(256)S(1)} %dynamic_slice.6), kind=kOutput, calls=%fused_computation.5 | convolution fusion | flops 1076232192 | bytes 19137536 | tf_op jit(solution)/shard_map/dot_general | solution.py:63
  76.7 179.3 %all-reduce.1 = bf16[4096,512]{0,1:T(8,128)(2,1)} all-reduce(f32[4096,512]{0,1:T(8,128)} %bitcast_multiply_fusion), channel_id=1, replica_groups=mesh['seq'=32,'head'=8] {'seq'}, use_global_device_ids=true, to_apply=%region_1.0 | all-reduce | flops 2097152 | bytes 12582912 | tf_op jit(solution)/shard_map/psum | solution.py:72
  256.0 7.0 %fusion.31 = f32[256,512]{1,0:T(8,128)S(1)} fusion(bf16[8192,512]{1,0:T(8,128)(2,1)} %all-gather.10.cloned.1.call-done, bf16[256,8192]{1,0:T(8,128)(2,1)} %param.9, f32[8192]{0:T(1024)S(1)} %copy-done.4, f32[256]{0:T(256)S(1)} %add_rsqrt_fusion), kind=kOutput, calls=%fused_computation.34 | convolution fusion | flops 2155872256 | bytes 13140992 | tf_op jit(solution)/shard_map/dot_general | solution.py:46
  263.0 13.7 %all-gather.14.cloned.1.call-done = bf16[256,4096]{1,0:T(8,128)(2,1)} async-done(((bf16[256,512]{1,0:T(8,128)(2,1)}), bf16[256,4096]{1,0:T(8,128)(2,1)}) %all-gather.14.cloned.1.call-update) | async-done | bytes 2097168 | tf_op jit(solution)/shard_map/all_gather | solution.py:59
  276.7 4.2 fusion.19
  280.9 75.8 %all-gather.8.cloned.1.call-done = bf16[8192,128]{1,0:T(8,128)(2,1)} async-done(((bf16[256,128]{1,0:T(8,128)(2,1)}), bf16[8192,128]{1,0:T(8,128)(2,1)}) %all-gather.8.cloned.1.call-update) | async-done | bytes 2097168 | tf_op jit(solution)/shard_map/all_gather | solution.py:52
  356.7 4.5 %fusion.37 = (f32[4,256]{1,0:T(4,128)S(1)}, f32[1,4,256,256]{2,3,1,0:T(8,128)S(1)}) fusion(bf16[32,4,8,128]{3,2,1,0:T(8,128)(2,1)S(1)} %fusion.19, bf16[8192,128]{1,0:T(8,128)(2,1)} %all-gather.8.cloned.1.call-done, bf16[256,8192]{1,0:T(8,128)(2,1)} %param.9, f32[8192]{0:T(1024)S(1)} %copy-done.4, f32[256]{0:T(256)S(1)} %add_rsqrt_fusion, ...), kind=kOutput, calls=%fused_computation.35 | convolution fusion | flops 613186560 | bytes 7705600 | tf_op jit(solution)/shard_map/pehm,qem->ehpq/dot_general | solution.py:16
  361.2 0.2 fusion.24
  361.3 74.5 %all-gather.6.cloned.1.call-done = bf16[8192,128]{1,0:T(8,128)(2,1)} async-done(((bf16[256,128]{1,0:T(8,128)(2,1)}), bf16[8192,128]{1,0:T(8,128)(2,1)}) %all-gather.6.cloned.1.call-update) | async-done | bytes 2097168 | tf_op jit(solution)/shard_map/all_gather | solution.py:56
  435.9 4.7 %convolution_convert_fusion = bf16[128,4,256]{2,0,1:T(8,128)(2,1)S(1)} fusion(bf16[8192,128]{1,0:T(8,128)(2,1)} %all-gather.6.cloned.1.call-done, f32[1,4,256,256]{2,3,1,0:T(8,128)S(1)} %get-tuple-element.6, f32[4,256]{1,0:T(4,128)S(1)} %fusion.24, f32[4,256]{1,0:T(4,128)S(1)} %get-tuple-element.5, bf16[256,8192]{1,0:T(8,128)(2,1)} %param.9, ...), kind=kOutput, calls=%fused_computation.14 | convolution fusion | flops 613318656 | bytes 7644160 | tf_op jit(solution)/shard_map/uczp,puv->zucv/dot_general | solution.py:27
  440.5 0.8 copy.19
  (17 shorter events, 0.2 us)
Async XLA Ops:
  6.5 3.4 copy-start
  6.5 6.7 %copy-start.3 = (s32[1,256]{1,0:T(1,128)S(1)}, s32[1,256]{1,0:T(1,128)}, u32[]{:S(2)}) copy-start(s32[1,256]{1,0:T(1,128)} %param.17) | copy-start | bytes 3076
  6.5 6.8 %copy-start.4 = (f32[8192]{0:T(1024)S(1)}, f32[8192]{0:T(1024)}, u32[]{:S(2)}) copy-start(f32[8192]{0:T(1024)} %param.10) | copy-start | bytes 98308
  6.5 59.4 %all-gather.12.cloned.1.call-start = ((), (), s32[]{:S(2)}) async-start(), calls=%async_computation.3 | async-start | bytes 2359296 | tf_op jit(solution)/shard_map/all_gather | solution.py:64
  7.3 248.7 %all-gather.10.cloned.1.call-start = ((), (), s32[]{:S(2)}) async-start(), calls=%async_computation.2 | async-start | bytes 8650752 | tf_op jit(solution)/shard_map/all_gather | solution.py:48
  8.0 268.7 %all-gather.14.cloned.1.call-start = ((), (), s32[]{:S(2)}) async-start(), calls=%async_computation.4 | async-start | bytes 2359296 | tf_op jit(solution)/shard_map/all_gather | solution.py:59
  8.7 347.9 %all-gather.8.cloned.1.call-start = ((), (), s32[]{:S(2)}) async-start(), calls=%async_computation.1 | async-start | bytes 2162688 | tf_op jit(solution)/shard_map/all_gather | solution.py:52
  9.3 426.5 %all-gather.6.cloned.1.call-start = ((), (), s32[]{:S(2)}) async-start(), calls=%async_computation | async-start | bytes 2162688 | tf_op jit(solution)/shard_map/all_gather | solution.py:56
  13.4 53.6 %copy-start.2 = (bf16[256,512]{1,0:T(8,128)(2,1)S(1)}, bf16[256,512]{1,0:T(8,128)(2,1)}, u32[]{:S(2)}) copy-start(bf16[256,512]{1,0:T(8,128)(2,1)} %param.13) | copy-start | bytes 786436
  65.9 1.6 copy-start.1
Sparse Core Ops, SparseCore 0:
  9.2 56.7 all-gather.11
  68.7 133.9 all-gather.9
  204.5 72.1 all-gather.13
  279.3 77.2 all-gather.7
  359.3 76.5 all-gather.5
where the time goes:
time: 448 us
  waiting for transfers between devices  220 us (49%)
  blocking collectives  179 us (40%)
  matrix products  29.5 us (7%)
  between operations  13.2 us (3%)
    psum x1, blocking collectives, local(): virtual = lax.psum(partial_virtual, 'seq').astype(jnp.bfloat16)  179 us
    all_gather x1, waiting for transfers between devices, local(): lax.all_gather(w_key, 'seq', axis=0, tiled=True)  75.8 us
    all_gather x1, waiting for transfers between devices, local(): lax.all_gather(w_value, 'seq', axis=0, tiled=True)  74.5 us
    all_gather x1, waiting for transfers between devices, local(): lax.all_gather(w_out1, 'head', axis=0, tiled=True)  52.5 us
    all_gather x1, waiting for transfers between devices, local(): sender_all = lax.all_gather(sender_diff, 'head', axis=1, tiled=True)  13.7 us
    dot_general x1, matrix products, local(): jnp.dot(lax.all_gather(w_out1, 'head', axis=0, tiled=True), scaled, prefe...  9.17 us
  transfers between devices with their start and end apart: 5, of which 4 were waited for; matrix products, arithmetic and copies ran while one was open for 7% of the time, Pallas kernels for 0%

commit v1 on v0

--- a/solution.py
+++ b/solution.py
@@ -53,7 +53,9 @@
     ).astype(jnp.bfloat16)
     values = jnp.dot(
         normed,
-        lax.all_gather(w_value, "seq", axis=0, tiled=True),
+        jnp.concatenate(
+            lax.all_to_all(jnp.stack([w_value] * lax.axis_size("seq")), "seq", 0, 0), axis=0
+        ),
         preferred_element_type=jnp.float32,
     ).astype(jnp.bfloat16)
     sender_all = lax.all_gather(sender_diff, "head", axis=1, tiled=True)

time: 448 us -> 395 us (0.88)
  waiting for transfers between devices: 220 us -> 153 us
  starting transfers between devices: 0.15 us -> 13 us
    all_gather x1 -> x0, waiting for transfers between devices: 74.5 us -> none  [local(): lax.all_gather(w_value, 'seq', axis=0, tiled=True)]
    all_to_all x0 -> x1, starting transfers between devices: none -> 12.9 us  [local(): lax.all_to_all(jnp.stack([w_value] * lax.axis_size('seq')), 'seq', 0, 0)]
    all_gather x1, waiting for transfers between devices: 52.5 us -> 61 us  [local(): lax.all_gather(w_out1, 'head', axis=0, tiled=True)]
  transfers between devices with their start and end apart: 5 -> 5, of which waited for: 4 -> 3; matrix products, arithmetic and copies ran while one was open for 7% -> 8% of each run, Pallas kernels for 0% -> 0%
where the time goes in v1:
time: 395 us
  blocking collectives  179 us (45%)
  waiting for transfers between devices  153 us (39%)
  matrix products  29 us (7%)
  between operations  13.2 us (3%)
  starting transfers between devices  13 us (3%)
  local copies, waits for them, and re-layouts  5.3 us (1%)
    psum x1, blocking collectives, local(): virtual = lax.psum(partial_virtual, 'seq').astype(jnp.bfloat16)  179 us
    all_gather x1, waiting for transfers between devices, local(): lax.all_gather(w_key, 'seq', axis=0, tiled=True)  76.1 us
    all_gather x1, waiting for transfers between devices, local(): lax.all_gather(w_out1, 'head', axis=0, tiled=True)  61 us
    all_to_all x1, starting transfers between devices, local(): lax.all_to_all(jnp.stack([w_value] * lax.axis_size('seq')), 'seq', 0, 0)  12.9 us
    all_gather x1, waiting for transfers between devices, local(): sender_all = lax.all_gather(sender_diff, 'head', axis=1, tiled=True)  12.8 us
    dot_general x1, matrix products, local(): jnp.dot(lax.all_gather(w_out1, 'head', axis=0, tiled=True), scaled, prefe...  9.2 us
  transfers between devices with their start and end apart: 5, of which 3 were waited for; matrix products, arithmetic and copies ran while one was open for 8% of the time, Pallas kernels for 0%

profile of v1, /device:TPU:1, one launch (start us, length us, event | category | flops | bytes accessed | tf_op | source)
XLA Modules:
  0.0 395.0 jit_solution(7619253311402323624)
XLA Ops:
  6.5 0.7 all-gather.9.cloned.1.call-update
  7.3 0.7 all-gather.7.cloned.1.call-update
  8.1 0.7 all-gather.11.cloned.1.call-update
  8.7 2.6 stack.2
  11.4 12.9 %all-to-all-start = ((bf16[32,256,128]{2,1,0:T(8,128)(2,1)}), bf16[32,256,128]{2,1,0:T(8,128)(2,1)S(1)}, u32[]{:S(2)}, u32[]{:S(2)}) async-start(bf16[32,256,128]{2,1,0:T(8,128)(2,1)} %stack.2), calls=%async_computation | async-start | bytes 4194304 | tf_op jit(solution)/shard_map/all_to_all | solution.py:57
  24.3 0.5 all-gather.5.cloned.1.call-update
  24.9 0.1 constant_dynamic-slice_fusion
  24.9 0.1 copy.22
  25.0 3.1 fusion
  28.2 0.1 fusion.30
  28.3 0.1 dynamic_slice.6
  28.4 61.0 %all-gather.9.cloned.1.call-done = bf16[4096,256]{1,0:T(8,128)(2,1)} async-done(((bf16[512,256]{1,0:T(8,128)(2,1)}), bf16[4096,256]{1,0:T(8,128)(2,1)}) %all-gather.9.cloned.1.call-update) | async-done | bytes 2097168 | tf_op jit(solution)/shard_map/all_gather | solution.py:66
  89.4 1.1 mul.77
  90.5 0.4 copy-done.1
  91.0 9.2 %bitcast_multiply_fusion = f32[4096,512]{0,1:T(8,128)} fusion(f32[64,8,32,128]{3,2,1,0:T(8,128)S(1)} %bitcast.55, bf16[4096,256]{1,0:T(8,128)(2,1)S(1)} %copy-done.1, bf16[256,512]{1,0:T(8,128)(2,1)S(1)} %copy-done.2, f32[256]{0:T(256)S(1)} %dynamic_slice.6), kind=kOutput, calls=%fused_computation.5 | convolution fusion | flops 1076232192 | bytes 19137536 | tf_op jit(solution)/shard_map/dot_general | solution.py:65
  100.2 178.5 %all-reduce.1 = bf16[4096,512]{0,1:T(8,128)(2,1)} all-reduce(f32[4096,512]{0,1:T(8,128)} %bitcast_multiply_fusion), channel_id=1, replica_groups=mesh['seq'=32,'head'=8] {'seq'}, use_global_device_ids=true, to_apply=%region_1.0 | all-reduce | flops 2097152 | bytes 12582912 | tf_op jit(solution)/shard_map/psum | solution.py:74
  278.7 7.1 %fusion.31 = f32[256,512]{1,0:T(8,128)S(1)} fusion(bf16[8192,512]{1,0:T(8,128)(2,1)} %all-gather.7.cloned.1.call-done, bf16[256,8192]{1,0:T(8,128)(2,1)} %param.9, f32[8192]{0:T(1024)S(1)} %copy-done.4, f32[256]{0:T(256)S(1)} %add_rsqrt_fusion), kind=kOutput, calls=%fused_computation.34 | convolution fusion | flops 2155872256 | bytes 13140992 | tf_op jit(solution)/shard_map/dot_general | solution.py:46
  285.8 12.8 %all-gather.11.cloned.1.call-done = bf16[256,4096]{1,0:T(8,128)(2,1)} async-done(((bf16[256,512]{1,0:T(8,128)(2,1)}), bf16[256,4096]{1,0:T(8,128)(2,1)}) %all-gather.11.cloned.1.call-update) | async-done | bytes 2097168 | tf_op jit(solution)/shard_map/all_gather | solution.py:61
  298.7 4.1 %fusion.19 = bf16[32,4,8,128]{3,2,1,0:T(8,128)(2,1)S(1)} fusion(f32[256,512]{1,0:T(8,128)S(1)} %fusion.31, bf16[256,4096]{1,0:T(8,128)(2,1)} %all-gather.11.cloned.1.call-done, bf16[4096,512]{0,1:T(8,128)(2,1)} %all-reduce.1, f32[256]{0:T(256)S(1)} %add_rsqrt_fusion), kind=kOutput, calls=%fused_computation.16 | convolution fusion | flops 1074135040 | bytes 7078912 | tf_op jit(solution)/shard_map/dot_general | solution.py:75
  302.8 76.1 %all-gather.5.cloned.1.call-done = bf16[8192,128]{1,0:T(8,128)(2,1)} async-done(((bf16[256,128]{1,0:T(8,128)(2,1)}), bf16[8192,128]{1,0:T(8,128)(2,1)}) %all-gather.5.cloned.1.call-update) | async-done | bytes 2097168 | tf_op jit(solution)/shard_map/all_gather | solution.py:52
  378.9 4.5 %fusion.37 = (f32[4,256]{1,0:T(4,128)S(1)}, f32[1,4,256,256]{2,3,1,0:T(8,128)S(1)}) fusion(bf16[32,4,8,128]{3,2,1,0:T(8,128)(2,1)S(1)} %fusion.19, bf16[8192,128]{1,0:T(8,128)(2,1)} %all-gather.5.cloned.1.call-done, bf16[256,8192]{1,0:T(8,128)(2,1)} %param.9, f32[8192]{0:T(1024)S(1)} %copy-done.4, f32[256]{0:T(256)S(1)} %add_rsqrt_fusion, ...), kind=kOutput, calls=%fused_computation.35 | convolution fusion | flops 613186560 | bytes 7705600 | tf_op jit(solution)/shard_map/pehm,qem->ehpq/dot_general | solution.py:16
  383.5 0.2 fusion.24
  383.6 4.0 %convolution_convert_fusion = bf16[128,4,256]{2,0,1:T(8,128)(2,1)S(1)} fusion(bf16[8192,128]{1,0:T(8,128)(2,1)S(1)} %bitcast.56, f32[1,4,256,256]{2,3,1,0:T(8,128)S(1)} %get-tuple-element.6, f32[4,256]{1,0:T(4,128)S(1)} %fusion.24, f32[4,256]{1,0:T(4,128)S(1)} %get-tuple-element.5, bf16[256,8192]{1,0:T(8,128)(2,1)} %param.9, f32[8192]{0:T(1024)S(1)} %copy-done.4, ...), kind=kOutput, calls=%fused_computation.14 | convolution fusion | flops 613318656 | bytes 7644160 | tf_op jit(solution)/shard_map/uczp,puv->zucv/dot_general | solution.py:27
  387.6 0.8 copy.19
  (17 shorter events, 0.2 us)
Async XLA Ops:
  6.5 18.3 %copy-start = (s32[32,32]{1,0:T(8,128)S(1)}, s32[32,32]{1,0:T(8,128)}, u32[]{:S(2)}) copy-start(s32[32,32]{1,0:T(8,128)} %param.16) | copy-start | bytes 12292
  6.5 82.9 %all-gather.9.cloned.1.call-start = ((), (), s32[]{:S(2)}) async-start(), calls=%async_computation.3 | async-start | bytes 2359296 | tf_op jit(solution)/shard_map/all_gather | solution.py:66
  7.3 271.5 %all-gather.7.cloned.1.call-start = ((), (), s32[]{:S(2)}) async-start(), calls=%async_computation.2 | async-start | bytes 8650752 | tf_op jit(solution)/shard_map/all_gather | solution.py:48
  8.0 290.6 %all-gather.11.cloned.1.call-start = ((), (), s32[]{:S(2)}) async-start(), calls=%async_computation.4 | async-start | bytes 2359296 | tf_op jit(solution)/shard_map/all_gather | solution.py:61
  11.4 16.8 %copy-start.3 = (s32[1,256]{1,0:T(1,128)S(1)}, s32[1,256]{1,0:T(1,128)}, u32[]{:S(2)}) copy-start(s32[1,256]{1,0:T(1,128)} %param.17) | copy-start | bytes 3076
  11.4 16.9 %copy-start.4 = (f32[8192]{0:T(1024)S(1)}, f32[8192]{0:T(1024)}, u32[]{:S(2)}) copy-start(f32[8192]{0:T(1024)} %param.10) | copy-start | bytes 98308
  11.4 372.2 %all-to-all-start = ((bf16[32,256,128]{2,1,0:T(8,128)(2,1)}), bf16[32,256,128]{2,1,0:T(8,128)(2,1)S(1)}, u32[]{:S(2)}, u32[]{:S(2)}) async-start(bf16[32,256,128]{2,1,0:T(8,128)(2,1)} %stack.2), calls=%async_computation | async-start | bytes 4194304 | tf_op jit(solution)/shard_map/all_to_all | solution.py:57
  24.3 354.7 %all-gather.5.cloned.1.call-start = ((), (), s32[]{:S(2)}) async-start(), calls=%async_computation.1 | async-start | bytes 2162688 | tf_op jit(solution)/shard_map/all_gather | solution.py:52
  28.4 62.2 %copy-start.2 = (bf16[256,512]{1,0:T(8,128)(2,1)S(1)}, bf16[256,512]{1,0:T(8,128)(2,1)}, u32[]{:S(2)}) copy-start(bf16[256,512]{1,0:T(8,128)(2,1)} %param.13) | copy-start | bytes 786436
  89.4 1.6 copy-start.1
Sparse Core Ops, SparseCore 0:
  9.1 80.2 all-gather.8
  92.2 133.8 all-gather.6
  227.9 70.7 all-gather.10
  301.3 77.6 all-gather.4
